TPU v7x, 128 devices: a whole 4x4x4 slice. The times are simulated.
128 devices in a mesh: dp: 4 (over x_lo, core), code: 32 (over z, y, x_hi).
Axes of the slice: x: 4 (x_hi: 2, x_lo: 2; x = x_hi * 2 + x_lo), y: 4, z: 4, core: 2. Of those that a mesh axis runs over, the one named last changes fastest.
Arguments:
- image_tokens: bfloat16 [16384, 1024], P(('dp', 'code')), may hold values from -6 to 6
- w_in: bfloat16 [1024, 4096], replicated, as said below
- w_out: bfloat16 [4096, 1024], replicated, as said below
- w_proj: bfloat16 [1024, 256], replicated, as said below
- codebook: bfloat16 [131072, 256], P('code'), may hold values from -6 to 6
- inv_temp: float32 [16384], replicated, may hold values from 4 to 240, as said below
- prior_mass: float32 [131072], P('code'), may hold values from 0.02 to 0.2
Outputs:
- refit_codes: float32 [131072, 256], P(('code', 'dp'))
- code_mass: float32 [131072], P(('code', 'dp'))
Inputs may be any that keep to these rules, and one draw needn't show every extreme that they name: `inv_temp`: positive inverse temperatures. `w_in`: every entry lies within 6 / sqrt(1024) of zero. `w_out`: every entry lies within 6 / sqrt(4096) of zero. `w_proj`: every entry lies within 6 / sqrt(1024) of zero.
All inputs are finite; a program needn't handle non-finite values.
Results may differ from a plain program's by a relative error of at most 0.003.
The roundings to bfloat16 on the way count: a program that leaves them out, or rounds other values in their place, can miss the bound.
Values may be sent and summed in bfloat16 or wider, within the bound.
A program may use at most 128 MiB of HBM per device.

v0:
```python
import math

import jax
import jax.numpy as jnp
from jax import lax
from jax.sharding import PartitionSpec as P


def encode(image_tokens, w_in, w_out, w_proj):
    tokens_f = image_tokens.astype(jnp.float32)
    mean = jnp.mean(tokens_f, axis=1, keepdims=True)
    centered = tokens_f - mean
    var = jnp.mean(centered * centered, axis=1, keepdims=True)
    normed = (centered * lax.rsqrt(var + 1e-06)).astype(jnp.bfloat16)
    hidden = jax.nn.gelu(
        jnp.dot(normed, w_in, preferred_element_type=jnp.float32), approximate=False
    ).astype(jnp.bfloat16)
    encoded = (tokens_f + jnp.dot(hidden, w_out, preferred_element_type=jnp.float32)).astype(
        jnp.bfloat16
    )
    projected = jnp.dot(encoded, w_proj, preferred_element_type=jnp.float32)
    width = projected.shape[1]
    factor = jnp.sqrt(width / (jnp.sum(projected * projected, axis=1, keepdims=True) + 1e-06))
    return (projected * factor).astype(jnp.bfloat16)


def in_blocks(func, arrays):
    rows = arrays[0].shape[0]
    block = math.gcd(rows, 512)
    shaped = tuple((item.reshape((rows // block, block) + item.shape[1:]) for item in arrays))
    results = lax.map(lambda items: func(*items), shaped)
    return jax.tree.map(lambda item: item.reshape((rows,) + item.shape[2:]), results)


def weighted_sums(token_rows, scale_rows, norm_rows, code_rows):
    rows = token_rows.shape[0]
    width = token_rows.shape[1]
    block = math.gcd(rows, 512)
    count = rows // block

    def accumulate(carry, items):
        token_block, scale_block, norm_block = items
        logits = (
            jnp.dot(token_block, code_rows.T, preferred_element_type=jnp.float32)
            * scale_block[:, None]
        )
        resp = jnp.exp(logits - norm_block[:, None]).astype(jnp.bfloat16)
        sums = carry[0] + lax.dot_general(
            resp, token_block, (((0,), (0,)), ((), ())), preferred_element_type=jnp.float32
        )
        mass = carry[1] + jnp.sum(resp.astype(jnp.float32), axis=0)
        return ((sums, mass), None)

    start = (
        jnp.zeros((code_rows.shape[0], width), jnp.float32),
        jnp.zeros((code_rows.shape[0],), jnp.float32),
    )
    items = (
        token_rows.reshape(count, block, width),
        scale_rows.reshape(count, block),
        norm_rows.reshape(count, block),
    )
    (sums, mass), _ = lax.scan(accumulate, start, items)
    return (sums, mass)


def local(image_tokens, w_in, w_out, w_proj, codebook, inv_temp, prior_mass):
    unit_tokens = encode(image_tokens, w_in, w_out, w_proj)
    width = unit_tokens.shape[1]
    codebook_f = codebook.astype(jnp.float32)
    unit_codes = (
        codebook_f * lax.rsqrt(jnp.mean(codebook_f * codebook_f, axis=1, keepdims=True) + 1e-06)
    ).astype(jnp.bfloat16)
    group_rows = unit_tokens.shape[0] * lax.axis_size("code")
    group_index = lax.axis_index("dp")
    all_scale = inv_temp * (1.0 / width)
    group_scale = lax.dynamic_slice_in_dim(all_scale, group_index * group_rows, group_rows)

    def block_stats(token_block, scale_block):
        logits = (
            jnp.dot(token_block, unit_codes.T, preferred_element_type=jnp.float32)
            * scale_block[:, None]
        )
        peak = jnp.max(logits, axis=1)
        return (peak, jnp.sum(jnp.exp(logits - peak[:, None]), axis=1))

    piece = lax.all_gather(unit_tokens, "code", axis=0, tiled=True)
    peak, total = in_blocks(block_stats, (piece, group_scale))
    local_peak = peak
    local_total = total
    peak = lax.pmax(local_peak, "code")
    total = lax.psum(local_total * jnp.exp(local_peak - peak), "code")
    lognorm = peak + jnp.log(total)
    owned = codebook.shape[0] // lax.axis_size("dp")
    sums, mass = weighted_sums(piece, group_scale, lognorm, unit_codes)
    sums, mass = (
        lax.psum_scatter(sums, "dp", scatter_dimension=0, tiled=True),
        lax.psum_scatter(mass, "dp", scatter_dimension=0, tiled=True),
    )
    own_book = lax.dynamic_slice_in_dim(codebook_f, group_index * owned, owned)
    own_prior = lax.dynamic_slice_in_dim(prior_mass, group_index * owned, owned)
    refit = (own_prior[:, None] * own_book + sums) / (own_prior + mass)[:, None]
    return (refit, mass)


def solution(mesh):
    placed = (P(("dp", "code"), None), P(), P(), P(), P("code", None), P(), P("code"))
    return jax.shard_map(
        local,
        mesh=mesh,
        in_specs=placed,
        out_specs=(P(("code", "dp"), None), P(("code", "dp"))),
        check_vma=False,
    )
```

profile of v0, /device:TPU:0, one launch (start us, length us, event | category | flops | bytes accessed | tf_op | source)
XLA Modules:
  0.0 664.6 jit_solution(4588213453708250442)
XLA Ops:
  7.2 1.1 convert_reduce_fusion.1
  8.3 1.0 convert_element_type.28
  9.4 1.2 fusion.26
  10.5 6.2 fusion.28
  16.7 1.6 broadcast.55
  18.3 1.6 erfc.269
  19.9 1.5 erfc.271
  21.4 1.5 erfc.274
  22.9 1.6 erfc.277
  24.5 1.6 erfc.280
  26.0 1.6 erfc.283
  27.6 1.6 erfc.286
  29.2 1.5 erfc.290
  30.8 1.6 erfc.292
  32.3 1.5 erfc.294
  33.8 1.5 erfc.301
  35.4 1.6 mul.100
  37.0 1.5 mul.98
  38.5 18.3 %multiply_reduce_fusion.2 = (f32[128]{0:T(128)S(1)}, f32[128,256]{1,0:T(8,128)S(1)}) fusion(bf16[1024,256]{1,0:T(8,128)(2,1)S(1)} %copy-done, f32[128,1024]{1,0:T(8,128)S(1)} %convert_element_type.28, bf16[4096,1024]{1,0:T(8,128)(2,1)} %param.13, f32[128,4096]{1,0:T(8,128)} %erfc.292, f32[128,4096]{1,0:T(8,128)} %erfc.290, f32[128,4096]{1,0:T(8,128)} %erfc.301, ...), kind=kOutput, calls=%fused_computation.54 | convolution fusion | flops 1175256960 | bytes 41026048 | tf_op jit(solution)/shard_map/dot_general | solution.py:21
  56.8 0.7 multiply_convert_fusion.1
  59.2 0.9 copy-done.3
  60.9 69.9 %all-gather.2.cloned.1.call-done = bf16[4096,256]{1,0:T(8,128)(2,1)} async-done(((bf16[128,256]{1,0:T(8,128)(2,1)}), bf16[4096,256]{1,0:T(8,128)(2,1)}) %all-gather.2.cloned.1.call-update) | async-done | bytes 2097168 | tf_op jit(solution)/shard_map/all_gather | solution.py:87
  130.8 34.2 %while.25 = (s32[]{:T(128)}, f32[8,512]{1,0:T(8,128)S(1)}, f32[8,512]{1,0:T(8,128)S(1)}, bf16[8,512,256]{2,1,0:T(8,128)(2,1)}, bf16[4096,256]{1,0:T(8,128)(2,1)S...) while((s32[]{:T(128)}, f32[8,512]{1,0:T(8,128)S(1)}, f32[8,512]{1,0:T(8,128)S(1)}, ...), condition=%wide.region_7.8_spmd, body=%wide.region_4.7_spmd.sunk | while | flops 1084226560 | bytes 19159648 | solution.py:31
  130.8 2.3 multiply_reduce_fusion.4
  133.1 1.8 exponential_reduce_fusion.2
  135.0 2.3 multiply_reduce_fusion.4
  137.4 1.8 exponential_reduce_fusion.2
  139.3 2.3 multiply_reduce_fusion.4
  141.6 1.8 exponential_reduce_fusion.2
  143.6 2.3 multiply_reduce_fusion.4
  145.9 1.8 exponential_reduce_fusion.2
  147.9 2.3 multiply_reduce_fusion.4
  150.2 1.8 exponential_reduce_fusion.2
  152.2 2.3 multiply_reduce_fusion.4
  154.5 1.8 exponential_reduce_fusion.2
  156.4 2.3 multiply_reduce_fusion.4
  158.8 1.8 exponential_reduce_fusion.2
  160.7 2.3 multiply_reduce_fusion.4
  163.0 1.8 exponential_reduce_fusion.2
  165.0 180.8 %pmax.7 = f32[4096]{0:T(1024)S(1)} all-reduce(f32[4096]{0:T(1024)S(1)} %bitcast.56), channel_id=1, replica_groups=mesh['dp'=4,'code'=32] {'code'}, use_global_device_ids=true, to_apply=%region_8.9 | all-reduce | flops 4096 | bytes 32768 | tf_op jit(solution)/shard_map/pmax | solution.py:91
  345.8 176.9 %psum.7 = f32[4096]{0:T(1024)S(1)} all-reduce(f32[4096]{0:T(1024)S(1)} %exponential_multiply_fusion), channel_id=1, replica_groups=mesh['dp'=4,'code'=32] {'code'}, use_global_device_ids=true, to_apply=%region_9.10 | all-reduce | flops 4096 | bytes 32768 | tf_op jit(solution)/shard_map/psum | solution.py:92
  522.7 91.9 %while.26 = (s32[]{:T(128)}, f32[4096,256]{1,0:T(8,128)}, f32[4096]{0:T(1024)S(1)}, bf16[8,512,256]{2,1,0:T(8,128)(2,1)}, bf16[4096,256]{1,0:T(8,128)(2,1)S(1)},...) while((s32[]{:T(128)}, f32[4096,256]{1,0:T(8,128)}, ...), condition=%wide.region_12.13_spmd.clone, body=%wide.region_10.12_spmd.clone.sunk | while | flops 2160070656 | bytes 19477612 | solution.py:63
  522.7 4.9 convert_reduce_fusion.3
  527.6 5.4 convolution_add_fusion.3
  533.1 4.9 convert_reduce_fusion.3
  537.9 6.8 %convolution_add_fusion.3 = f32[4096,256]{1,0:T(8,128)} fusion(bf16[512,4096]{1,0:T(8,128)(2,1)} %get-tuple-element.228, f32[4096,256]{1,0:T(8,128)} %get-tuple-element.264, pred[]{:T(512)S(6)} %compare.3, bf16[8,512,256]{2,1,0:T(8,128)(2,1)} %get-tuple-element.275, s32[]{:T(128)} %get-tuple-element.263), kind=kOutput, calls=%fused_computation.9.clone.1 | convolution fusion | flops 1075838976 | bytes 12845569 | tf_op jit(solution)/shard_map/while/body/eval_jaxpr/dot_general | solution.py:48
  544.7 4.9 convert_reduce_fusion.3
  549.6 6.8 %convolution_add_fusion.3 = f32[4096,256]{1,0:T(8,128)} fusion(bf16[512,4096]{1,0:T(8,128)(2,1)} %get-tuple-element.228, f32[4096,256]{1,0:T(8,128)} %get-tuple-element.264, pred[]{:T(512)S(6)} %compare.3, bf16[8,512,256]{2,1,0:T(8,128)(2,1)} %get-tuple-element.275, s32[]{:T(128)} %get-tuple-element.263), kind=kOutput, calls=%fused_computation.9.clone.1 | convolution fusion | flops 1075838976 | bytes 12845569 | tf_op jit(solution)/shard_map/while/body/eval_jaxpr/dot_general | solution.py:48
  556.4 4.9 convert_reduce_fusion.3
  561.2 6.8 %convolution_add_fusion.3 = f32[4096,256]{1,0:T(8,128)} fusion(bf16[512,4096]{1,0:T(8,128)(2,1)} %get-tuple-element.228, f32[4096,256]{1,0:T(8,128)} %get-tuple-element.264, pred[]{:T(512)S(6)} %compare.3, bf16[8,512,256]{2,1,0:T(8,128)(2,1)} %get-tuple-element.275, s32[]{:T(128)} %get-tuple-element.263), kind=kOutput, calls=%fused_computation.9.clone.1 | convolution fusion | flops 1075838976 | bytes 12845569 | tf_op jit(solution)/shard_map/while/body/eval_jaxpr/dot_general | solution.py:48
  568.0 4.9 convert_reduce_fusion.3
  572.9 6.8 %convolution_add_fusion.3 = f32[4096,256]{1,0:T(8,128)} fusion(bf16[512,4096]{1,0:T(8,128)(2,1)} %get-tuple-element.228, f32[4096,256]{1,0:T(8,128)} %get-tuple-element.264, pred[]{:T(512)S(6)} %compare.3, bf16[8,512,256]{2,1,0:T(8,128)(2,1)} %get-tuple-element.275, s32[]{:T(128)} %get-tuple-element.263), kind=kOutput, calls=%fused_computation.9.clone.1 | convolution fusion | flops 1075838976 | bytes 12845569 | tf_op jit(solution)/shard_map/while/body/eval_jaxpr/dot_general | solution.py:48
  579.7 4.9 convert_reduce_fusion.3
  584.5 6.8 %convolution_add_fusion.3 = f32[4096,256]{1,0:T(8,128)} fusion(bf16[512,4096]{1,0:T(8,128)(2,1)} %get-tuple-element.228, f32[4096,256]{1,0:T(8,128)} %get-tuple-element.264, pred[]{:T(512)S(6)} %compare.3, bf16[8,512,256]{2,1,0:T(8,128)(2,1)} %get-tuple-element.275, s32[]{:T(128)} %get-tuple-element.263), kind=kOutput, calls=%fused_computation.9.clone.1 | convolution fusion | flops 1075838976 | bytes 12845569 | tf_op jit(solution)/shard_map/while/body/eval_jaxpr/dot_general | solution.py:48
  591.3 4.9 convert_reduce_fusion.3
  596.2 6.8 %convolution_add_fusion.3 = f32[4096,256]{1,0:T(8,128)} fusion(bf16[512,4096]{1,0:T(8,128)(2,1)} %get-tuple-element.228, f32[4096,256]{1,0:T(8,128)} %get-tuple-element.264, pred[]{:T(512)S(6)} %compare.3, bf16[8,512,256]{2,1,0:T(8,128)(2,1)} %get-tuple-element.275, s32[]{:T(128)} %get-tuple-element.263), kind=kOutput, calls=%fused_computation.9.clone.1 | convolution fusion | flops 1075838976 | bytes 12845569 | tf_op jit(solution)/shard_map/while/body/eval_jaxpr/dot_general | solution.py:48
  603.0 4.9 convert_reduce_fusion.3
  607.8 6.8 %convolution_add_fusion.3 = f32[4096,256]{1,0:T(8,128)} fusion(bf16[512,4096]{1,0:T(8,128)(2,1)} %get-tuple-element.228, f32[4096,256]{1,0:T(8,128)} %get-tuple-element.264, pred[]{:T(512)S(6)} %compare.3, bf16[8,512,256]{2,1,0:T(8,128)(2,1)} %get-tuple-element.275, s32[]{:T(128)} %get-tuple-element.263), kind=kOutput, calls=%fused_computation.9.clone.1 | convolution fusion | flops 1075838976 | bytes 12845569 | tf_op jit(solution)/shard_map/while/body/eval_jaxpr/dot_general | solution.py:48
  614.6 1.6 copy-done.4
  616.2 2.4 convert_element_type.27
  619.9 11.8 %all-reduce = f32[4096]{0:T(1024)S(1)} all-reduce(f32[4096]{0:T(1024)S(1)} %get-tuple-element.76), channel_id=3, replica_groups=mesh['dp'=4,'code'=32] {'dp'}, use_global_device_ids=true, to_apply=%region_14.15.clone | all-reduce | flops 4096 | bytes 32768
  631.6 1.3 fusion.64
  632.9 22.0 %reduce-scatter.2.cloned.1.call-done = f32[1024,256]{1,0:T(8,128)} async-done(((f32[4096,256]{1,0:T(8,128)}), f32[1024,256]{1,0:T(8,128)}) %reduce-scatter.2.cloned.1.call-update) | async-done | bytes 1048592 | tf_op jit(solution)/shard_map/reduce_scatter | solution.py:97
  654.9 2.8 add_divide_fusion
  (72 shorter events, 4.1 us)
Async XLA Ops:
  7.2 31.3 %copy-start = (bf16[1024,256]{1,0:T(8,128)(2,1)S(1)}, bf16[1024,256]{1,0:T(8,128)(2,1)}, u32[]{:S(2)}) copy-start(bf16[1024,256]{1,0:T(8,128)(2,1)} %param.14) | copy-start | bytes 1572868
  7.2 123.6 %all-gather.2.cloned.1.call-start = ((), (), s32[]{:S(2)}) async-start(), calls=%async_computation.1 | async-start | bytes 2162688 | tf_op jit(solution)/shard_map/all_gather | solution.py:87
  38.5 20.1 %copy-start.2 = (bf16[4096,256]{1,0:T(8,128)(2,1)S(1)}, bf16[4096,256]{1,0:T(8,128)(2,1)}, u32[]{:S(2)}) copy-start(bf16[4096,256]{1,0:T(8,128)(2,1)} %param.15) | copy-start | bytes 6291460
  57.6 597.3 %reduce-scatter.2.cloned.1.call-start = ((), (), s32[]{:S(2)}) async-start(), calls=%async_computation.2 | async-start | bytes 5242880 | tf_op jit(solution)/shard_map/reduce_scatter | solution.py:97
  58.6 1.6 copy-start.3
  614.6 1.6 copy-start.4
  616.2 2.4 copy-start.5
  616.2 41.6 %copy-start.1 = (bf16[1024,256]{1,0:T(8,128)(2,1)S(1)}, bf16[1024,256]{1,0:T(8,128)(2,1)}, u32[]{:S(2)}) copy-start(bf16[1024,256]{1,0:T(8,128)(2,1)} %param.14) | copy-start | bytes 1572868
Sparse Core Ops, SparseCore 0:
  57.7 73.0 all-gather.1
  614.7 40.1 reduce-scatter.1
where the time goes:
time: 667 us; the launch traced here: 665 us
  blocking collectives  369 us (55%)
  matrix products  135 us (20%)
  waiting for transfers between devices  91.9 us (14%)
  other arithmetic  27 us (4%)
  local copies, waits for them, and re-layouts  25.9 us (4%)
  between operations  14.8 us (2%)
    pmax x1, blocking collectives, local(): peak = lax.pmax(local_peak, 'code')  181 us
    psum x1, blocking collectives, local(): total = lax.psum(local_total * jnp.exp(local_peak - peak), 'code')  177 us
    all_gather x1, waiting for transfers between devices, local(): piece = lax.all_gather(unit_tokens, 'code', axis=0, tiled=True)  69.9 us
    dot_general x8, matrix products, accumulate(): lax.dot_general(resp, token_block, (((0,), (0,)), ((), ())), preferred_el...  52.8 us
    dot_general x8, matrix products, accumulate(): jnp.dot(token_block, code_rows.T, preferred_element_type=jnp.float32)  38.9 us
    reduce_scatter x1, waiting for transfers between devices, local(): lax.psum_scatter(sums, 'dp', scatter_dimension=0, tiled=True)  22 us
    dot_general x8, matrix products, block_stats(): jnp.dot(token_block, unit_codes.T, preferred_element_type=jnp.float32)  18.6 us
    dot_general x1, matrix products, encode(): projected = jnp.dot(encoded, w_proj, preferred_element_type=jnp.float32)  18.3 us
  transfers between devices with their start and end apart: 2, of which 2 were waited for; matrix products, arithmetic and copies ran while one was open for 1% of the time, Pallas kernels for 0%

commit v1 on v0

v1 whole, which is shorter than its diff:
```python
import functools

import jax
import jax.numpy as jnp
from jax import lax
from jax.experimental import pallas as pl
from jax.experimental.pallas import tpu as pltpu
from jax.sharding import PartitionSpec as P

LOG2E = 1.4426950408889634
F32 = jnp.float32
BF16 = jnp.bfloat16
FT = 512
CH = 512
CB = 512
VMEM_LIMIT = 67043328


def encode_kernel(x_ref, win_ref, wout_ref, wproj_ref, o_ref, normed, acc):
    step = pl.program_id(0)

    @pl.when(step == 0)
    def _():
        x = x_ref[...].astype(F32)
        mean = jnp.mean(x, axis=1, keepdims=True)
        centered = x - mean
        var = jnp.mean(centered * centered, axis=1, keepdims=True)
        normed[...] = (centered * lax.rsqrt(var + 1e-06)).astype(BF16)
        acc[...] = jnp.zeros_like(acc)

    h = jnp.dot(normed[...], win_ref[...], preferred_element_type=F32)
    h = (0.5 * h * (1.0 + lax.erf(h * 0.7071067811865476))).astype(BF16)
    acc[...] += jnp.dot(h, wout_ref[...], preferred_element_type=F32)

    @pl.when(step == pl.num_programs(0) - 1)
    def _():
        encoded = (x_ref[...].astype(F32) + acc[...]).astype(BF16)
        projected = jnp.dot(encoded, wproj_ref[...], preferred_element_type=F32)
        width = projected.shape[1]
        factor = jnp.sqrt(width / (jnp.sum(projected * projected, axis=1, keepdims=True) + 1e-06))
        o_ref[...] = (projected * factor).astype(BF16)


def encode(x, w_in, w_out, w_proj):
    rows, d = x.shape
    ff, e = w_in.shape[1], w_proj.shape[1]
    return pl.pallas_call(
        encode_kernel,
        grid=(ff // FT,),
        in_specs=[
            pl.BlockSpec((rows, d), lambda i: (0, 0)),
            pl.BlockSpec((d, FT), lambda i: (0, i)),
            pl.BlockSpec((FT, d), lambda i: (i, 0)),
            pl.BlockSpec((d, e), lambda i: (0, 0)),
        ],
        out_specs=pl.BlockSpec((rows, e), lambda i: (0, 0)),
        out_shape=jax.ShapeDtypeStruct((rows, e), BF16),
        scratch_shapes=[pltpu.VMEM((rows, d), BF16), pltpu.VMEM((rows, d), F32)],
        name="encode",
    )(x, w_in, w_out, w_proj)


ORDER_A = [(0, 0), (1, 0), (3, 0), (0, 1), (1, 1), (3, 1), (2, 0), (2, 1)]
ORDER_B = [(0, 0), (0, 1), (1, 0), (1, 1), (3, 0), (3, 1), (2, 0), (2, 1)]


def pick(i, values):
    out = i * 0 + values[0]
    for k, v in enumerate(values[1:], 1):
        out = out + (i == k).astype(jnp.int32) * (v - values[0])
    return out


def refit_kernel(
    ut_ref, book_ref, inv_ref, prior_ref,
    out_ref, mass_ref,
    u_all, codes, p, ls0, ls1, lse, mloc, lx, ly, lz, u2,
    rc, rcm, rx, rxm, sx, sm, totals,
    ag_send, ag_recv, st_send, st_recv, rs_send, rs_recv,
):
    n_codes, width = book_ref.shape
    n_blocks = 16
    tb_size = 256
    dp = lax.axis_index("dp")
    code = lax.axis_index("code")
    h = lax.rem(code, 2)
    y = lax.rem(code // 2, 4)
    z = code // 8
    core = lax.rem(dp, 2)
    xlo = dp // 2

    zs = [lax.rem(z + d, 4) for d in range(4)]
    ys = [lax.rem(y + d, 4) for d in range(4)]

    def at(dz, dy, flip=0):
        hh = 1 - h if flip else h
        return (dp, (zs[dz] * 4 + ys[dy]) * 2 + hh)

    partner = (xlo * 2 + (1 - core), code)
    across = ((1 - xlo) * 2 + core, code)

    barrier = pltpu.get_barrier_semaphore()
    peers = [at(0, 0, 1), partner, across]
    peers += [at(d, 0) for d in (1, 2, 3)] + [at(0, d) for d in (1, 2, 3)]
    for peer in peers:
        pl.semaphore_signal(barrier, inc=1, device_id=peer, device_id_type=pl.DeviceIdType.MESH)
    pl.semaphore_wait(barrier, len(peers))

    sent = []

    def place(color, dz, dy):
        return color * 16 + zs[dz % 4] * 4 + ys[dy % 4]

    def view(index, half):
        if half is None:
            return u_all.at[index]
        return u_all.at[index, pl.ds(64 * half, 64)]

    def copy(src, dst, color, dz, dy, half, to):
        slot = ((color * 4 + dz % 4) * 4 + dy % 4) * 2 + (half or 0)
        c = pltpu.make_async_remote_copy(
            src_ref=src, dst_ref=dst, send_sem=ag_send.at[len(sent)], recv_sem=ag_recv.at[slot],
            device_id=to, device_id_type=pl.DeviceIdType.MESH,
        )
        sent.append(half)
        c.start()

    def send(color, dz, dy, half, ez, ey):
        ref = view(place(color, dz, dy), half)
        copy(ref, ref, color, dz - ez, dy - ey, half, at(ez % 4, ey % 4))

    def arrived(color, dz, dy, half=None):
        slot = ((color * 4 + dz) * 4 + dy) * 2 + (half or 0)
        ref = view(place(color, dz, dy), half)
        pltpu.make_async_remote_copy(
            src_ref=ref, dst_ref=ref, send_sem=ag_send.at[0], recv_sem=ag_recv.at[slot],
            device_id=at(1, 0), device_id_type=pl.DeviceIdType.MESH,
        ).wait_recv()

    def both(color, dz, dy, axis):
        for sign in (1, -1):
            send(color, dz, dy, None, *((sign, 0) if axis == "z" else (0, sign)))

    def onward(color, dz, dy, axis):
        arrived(color, dz, dy)
        step = dz if axis == "z" else dy
        half, sign = (0, -1) if step == 1 else (1, 1)
        send(color, dz, dy, half, *((sign, 0) if axis == "z" else (0, sign)))

    def halves(color, dz, dy):
        arrived(color, dz, dy, 0)
        arrived(color, dz, dy, 1)

    def c_start():
        ref = view(place(0, 0, 0), None)
        own = pltpu.make_async_copy(ut_ref, ref, rs_send.at[0])
        own.start()
        own.wait()
        copy(ref, view(place(1, 0, 0), None), 1, 0, 0, None, at(0, 0, 1))
        both(0, 0, 0, "y")
        both(0, 0, 0, "z")

    def c_first():
        for d in (1, 3):
            onward(0, 0, d, "y")
        for d in (1, 3):
            onward(0, d, 0, "z")
            both(0, d, 0, "y")

    def c0():
        arrived(1, 0, 0)
        both(1, 0, 0, "y")
        both(1, 0, 0, "z")
        for d in (1, 3):
            onward(0, 1, d, "y")

    def c1():
        for d in (1, 3):
            onward(0, 3, d, "y")
        halves(0, 2, 0)
        both(0, 2, 0, "y")

    def c2():
        halves(0, 0, 2)
        for d in (1, 3):
            onward(1, 0, d, "y")
            both(1, 0, d, "z")
        for d in (1, 3):
            onward(1, d, 0, "z")

    def c3():
        halves(0, 1, 2)

    def c4():
        halves(0, 3, 2)
        for d in (1, 3):
            onward(0, 2, d, "y")
        halves(1, 0, 2)
        both(1, 0, 2, "z")

    def c5():
        for e in (1, 3):
            for d in (1, 3):
                onward(1, e, d, "z")

    def c6():
        halves(0, 2, 2)

    def c7():
        for e in (1, 3):
            onward(1, e, 2, "z")

    def c13():
        halves(1, 2, 0)
        halves(1, 2, 1)
        halves(1, 2, 3)

    def c14():
        halves(1, 2, 2)

    comm = {0: c0, 1: c1, 2: c2, 3: c3, 4: c4, 5: c5, 6: c6, 7: c7, 13: c13, 14: c14}

    c_start()

    def unit_body(i, _):
        r = pl.ds(pl.multiple_of(i * 256, 256), 256)
        b = book_ref[r, :].astype(F32)
        codes[r, :] = (b * lax.rsqrt(jnp.mean(b * b, axis=1, keepdims=True) + 1e-06)).astype(BF16)
        return 0

    lax.fori_loop(0, n_codes // 256, unit_body, 0)
    c_first()

    rel_z = [a for a, _ in ORDER_A + ORDER_B]
    rel_p = [b for _, b in ORDER_A + ORDER_B]

    def block_at(i):
        color = i // 8
        zz = lax.rem(z + pick(i, rel_z), 4)
        pair = lax.rem(y // 2 + pick(i, rel_p), 2)
        hh = jnp.where(color == 0, h, 1 - h)
        return color * 8 + zz * 2 + pair, dp * 32 + (zz * 4 + pair * 2) * 2 + hh

    neg = jnp.full((8, tb_size), -jnp.inf, F32)

    def logits_of(tb, q, dest, peak):
        tokens = u_all[pl.ds(2 * tb, 2)].reshape(tb_size, width)
        l = lax.dot_general(
            codes[q * CH:(q + 1) * CH, :], tokens, (((1,), (1,)), ((), ())), preferred_element_type=F32
        )
        dest[q * CH:(q + 1) * CH, :] = l
        return jnp.maximum(peak, jnp.max(l.reshape(CH // 8, 8, tb_size), axis=0))

    def step(i, peak8, cur, nxt):
        tb, row = block_at(i)
        nxt_tb, _ = block_at(jnp.minimum(i + 1, n_blocks - 1))
        scale = jnp.concatenate([inv_ref[pl.ds(row, 1), :], inv_ref[pl.ds(row + 2, 1), :]], axis=1)
        scale = scale * (LOG2E / width)
        peak = jnp.max(peak8, axis=0, keepdims=True) * scale
        columns = pl.ds(pl.multiple_of(tb * tb_size, tb_size), tb_size)
        new_peak = neg
        total = jnp.zeros((8, tb_size), F32)
        for q in range(n_codes // CH):
            new_peak = logits_of(nxt_tb, q, nxt, new_peak)
            e = jnp.exp2(cur[q * CH:(q + 1) * CH, :] * scale - peak)
            p[q * CH:(q + 1) * CH, columns] = e.astype(BF16)
            total = total + jnp.sum(e.reshape(CH // 8, 8, tb_size), axis=0)
        mloc[tb] = peak
        lse[tb] = peak + jnp.log2(jnp.sum(total, axis=0, keepdims=True))
        return new_peak

    first, _ = block_at(h * 0)
    peak = neg
    for q in range(n_codes // CH):
        peak = logits_of(first, q, ls0, peak)

    def two_steps(j, peak8):
        for s, (cur, nxt) in enumerate(((ls0, ls1), (ls1, ls0))):
            for k, fn in comm.items():
                if k % 2 == s:
                    pl.when(j == k // 2)(fn)
            peak8 = step(2 * j + s, peak8, cur, nxt)
        return peak8

    lax.fori_loop(0, n_blocks // 2, two_steps, peak)

    stat_sent = []

    def stat_send(src, dst, slot, to):
        c = pltpu.make_async_remote_copy(
            src_ref=src, dst_ref=dst, send_sem=st_send.at[slot], recv_sem=st_recv.at[slot],
            device_id=to, device_id_type=pl.DeviceIdType.MESH,
        )
        stat_sent.append(c)
        c.start()
        return c

    cx = [
        stat_send(lse.at[pl.ds(0, 8)], lx.at[pl.ds(8, 8)], 0, at(0, 0, 1)),
        stat_send(lse.at[pl.ds(8, 8)], lx.at[pl.ds(0, 8)], 1, at(0, 0, 1)),
    ]
    for c in cx:
        c.wait()
    parts = [lse[...], lx[...]]
    top = jnp.maximum(*parts)
    ly[0] = top + jnp.log2(sum(jnp.exp2(v - top) for v in parts))
    cy = [stat_send(ly.at[0], ly.at[d], 1 + d, at(0, d)) for d in (1, 2, 3)]
    for c in cy:
        c.wait()
    parts = [ly[d] for d in range(4)]
    top = functools.reduce(jnp.maximum, parts)
    lz[0] = top + jnp.log2(sum(jnp.exp2(v - top) for v in parts))
    cz = [stat_send(lz.at[0], lz.at[d], 4 + d, at(d, 0)) for d in (1, 2, 3)]
    for c in cz:
        c.wait()
    parts = [lz[d] for d in range(4)]
    top = functools.reduce(jnp.maximum, parts)
    mloc[...] = jnp.exp2(mloc[...] - (top + jnp.log2(sum(jnp.exp2(v - top) for v in parts))))

    for k, half in enumerate(sent):
        ref = view(place(0, 0, 0), half)
        pltpu.make_async_remote_copy(
            src_ref=ref, dst_ref=ref, send_sem=ag_send.at[k], recv_sem=ag_recv.at[0],
            device_id=at(1, 0), device_id_type=pl.DeviceIdType.MESH,
        ).wait_send()

    def scale_body(tb, _):
        w = jnp.broadcast_to(mloc[tb], (128, tb_size)).T
        w = jnp.concatenate([w, w], axis=1)
        rows = pl.ds(pl.multiple_of(tb * tb_size, tb_size), tb_size)
        tokens = u_all[pl.ds(2 * tb, 2)].reshape(tb_size, width)
        u2[rows, :] = (tokens.astype(F32) * w).astype(BF16)
        return 0

    lax.fori_loop(0, n_blocks, scale_body, 0)

    ones = jnp.ones((8, 128), F32)
    per = n_codes // 4
    subs = per // CB

    def sums_of(first_row):
        r = pl.ds(pl.multiple_of(first_row, CB), CB)
        s = jnp.dot(p[r, :], u2[...], preferred_element_type=F32)
        acc = jnp.zeros((CB, 128), F32)
        for j in range(n_blocks * 2):
            acc = acc + p[r, j * 128:(j + 1) * 128].astype(F32) * mloc[j // 2][:, (j % 2) * 128:(j % 2) * 128 + 128]
        m = lax.dot_general(
            ones, acc, (((1,), (1,)), ((), ())), preferred_element_type=F32, precision=lax.Precision.HIGHEST
        )
        return s, m

    def reduce_send(src, dst, slot, to):
        c = pltpu.make_async_remote_copy(
            src_ref=src, dst_ref=dst, send_sem=rs_send.at[slot], recv_sem=rs_recv.at[slot],
            device_id=to, device_id_type=pl.DeviceIdType.MESH,
        )
        c.start()
        return c

    stage = ls0

    for side in range(2):
        chip = (1 - xlo) if side == 0 else xlo
        theirs = (chip * 2 + (1 - core)) * per
        ours = (chip * 2 + core) * per

        def side_body(b, _, side=side, theirs=theirs, ours=ours):
            slot = side * subs + b
            rows = pl.ds(pl.multiple_of(slot * CB, CB), CB)
            s, m = sums_of(theirs + b * CB)
            stage[rows, :] = s
            sm[slot] = m
            c1 = reduce_send(stage.at[rows], rc.at[slot], slot, partner)
            c2 = reduce_send(sm.at[slot], rcm.at[slot], 4 + slot, partner)
            s, m = sums_of(ours + b * CB)
            c1.wait_recv()
            c2.wait_recv()
            s = s + rc[slot]
            m = m + rcm[slot]
            if side == 0:
                sx[b] = s.astype(BF16)
                sm[4 + b] = m
                reduce_send(sx.at[b], rx.at[b], 8 + b, across)
                reduce_send(sm.at[4 + b], rxm.at[b], 10 + b, across)
            else:
                totals[b] = s
                sm[4 + subs + b] = m
            return 0

        lax.fori_loop(0, subs, side_body, 0)

    def column(row):
        c = jnp.broadcast_to(row, (128, 128)).T
        return jnp.concatenate([c, c], axis=1)

    for b in range(subs):
        pltpu.make_async_remote_copy(
            src_ref=sx.at[b], dst_ref=rx.at[b], send_sem=rs_send.at[8 + b], recv_sem=rs_recv.at[8 + b],
            device_id=across, device_id_type=pl.DeviceIdType.MESH).wait_recv()
        pltpu.make_async_remote_copy(
            src_ref=sm.at[4 + b], dst_ref=rxm.at[b], send_sem=rs_send.at[10 + b], recv_sem=rs_recv.at[10 + b],
            device_id=across, device_id_type=pl.DeviceIdType.MESH).wait_recv()
        m = sm[4 + subs + b] + rxm[b]
        for k in range(CB // 128):
            local = b * CB + k * 128
            part = slice(k * 128, (k + 1) * 128)
            index = b * (CB // 128) + k
            m_row = m[0:1, part]
            mass_ref[index:index + 1, :] = m_row
            prior = column(prior_ref[pl.ds(dp * (per // 128) + index, 1), :])
            book = book_ref[pl.ds(pl.multiple_of(dp * per + local, 128), 128), :].astype(F32)
            s = totals[b, part, :] + rx[b, part, :].astype(F32)
            out_ref[local:local + 128, :] = (prior * book + s) / (prior + column(m_row))

    for slot in range(2 * subs):
        pltpu.make_async_remote_copy(
            src_ref=stage.at[pl.ds(slot * CB, CB)], dst_ref=rc.at[slot], send_sem=rs_send.at[slot],
            recv_sem=rs_recv.at[slot], device_id=partner, device_id_type=pl.DeviceIdType.MESH).wait_send()
        pltpu.make_async_remote_copy(
            src_ref=sm.at[slot], dst_ref=rcm.at[slot], send_sem=rs_send.at[4 + slot],
            recv_sem=rs_recv.at[4 + slot], device_id=partner, device_id_type=pl.DeviceIdType.MESH).wait_send()
    for b in range(subs):
        pltpu.make_async_remote_copy(
            src_ref=sx.at[b], dst_ref=rx.at[b], send_sem=rs_send.at[8 + b], recv_sem=rs_recv.at[8 + b],
            device_id=across, device_id_type=pl.DeviceIdType.MESH).wait_send()
        pltpu.make_async_remote_copy(
            src_ref=sm.at[4 + b], dst_ref=rxm.at[b], send_sem=rs_send.at[10 + b], recv_sem=rs_recv.at[10 + b],
            device_id=across, device_id_type=pl.DeviceIdType.MESH).wait_send()


def refit(unit_tokens, codebook, inv_temp, prior_mass):
    n_codes, width = codebook.shape
    tokens = unit_tokens.shape[0] * 32
    per = n_codes // 4
    subs = per // CB
    vmem = pl.BlockSpec(memory_space=pltpu.VMEM)
    out, mass = pl.pallas_call(
        refit_kernel,
        in_specs=[vmem] * 4,
        out_specs=[vmem] * 2,
        out_shape=[
            jax.ShapeDtypeStruct((per, width), F32),
            jax.ShapeDtypeStruct((per // 128, 128), F32),
        ],
        scratch_shapes=[
            pltpu.VMEM((32, 128, width), BF16),
            pltpu.VMEM((n_codes, width), BF16),
            pltpu.VMEM((n_codes, tokens), BF16),
            pltpu.VMEM((n_codes, 256), F32),
            pltpu.VMEM((n_codes, 256), F32),
            pltpu.VMEM((16, 1, 256), F32),
            pltpu.VMEM((16, 1, 256), F32),
            pltpu.VMEM((16, 1, 256), F32),
            pltpu.VMEM((4, 16, 1, 256), F32),
            pltpu.VMEM((4, 16, 1, 256), F32),
            pltpu.VMEM((tokens, width), BF16),
            pltpu.VMEM((2 * subs, CB, width), F32),
            pltpu.VMEM((2 * subs, 8, CB), F32),
            pltpu.VMEM((subs, CB, width), BF16),
            pltpu.VMEM((subs, 8, CB), F32),
            pltpu.VMEM((subs, CB, width), BF16),
            pltpu.VMEM((4 + 2 * subs, 8, CB), F32),
            pltpu.VMEM((subs, CB, width), F32),
            pltpu.SemaphoreType.DMA((48,)),
            pltpu.SemaphoreType.DMA((64,)),
            pltpu.SemaphoreType.DMA((8,)),
            pltpu.SemaphoreType.DMA((8,)),
            pltpu.SemaphoreType.DMA((12,)),
            pltpu.SemaphoreType.DMA((12,)),
        ],
        compiler_params=pltpu.CompilerParams(
            collective_id=0, has_side_effects=True, vmem_limit_bytes=VMEM_LIMIT
        ),
        name="refit",
    )(unit_tokens, codebook, inv_temp.reshape(-1, 128), prior_mass.reshape(-1, 128))
    return out, mass.reshape(-1)


def local(image_tokens, w_in, w_out, w_proj, codebook, inv_temp, prior_mass):
    unit_tokens = encode(image_tokens, w_in, w_out, w_proj)
    return refit(unit_tokens, codebook, inv_temp, prior_mass)


def solution(mesh):
    placed = (P(("dp", "code"), None), P(), P(), P(), P("code", None), P(), P("code"))
    return jax.shard_map(
        local,
        mesh=mesh,
        in_specs=placed,
        out_specs=(P(("code", "dp"), None), P(("code", "dp"))),
        check_vma=False,
    )
```

time: 667 us -> 103 us (0.15)
  blocking collectives: 369 us -> 0 us
  matrix products: 135 us -> 0 us
  Pallas kernels: 0 us -> 98.3 us
  waiting for transfers between devices: 91.9 us -> 0 us
  other arithmetic: 27 us -> 0 us
  local copies, waits for them, and re-layouts: 25.9 us -> 3.53 us
  between operations: 14.8 us -> 0.64 us
    pmax x1 -> x0, blocking collectives: 181 us -> none  [local(): peak = lax.pmax(local_peak, 'code')]
    psum x1 -> x0, blocking collectives: 177 us -> none  [local(): total = lax.psum(local_total * jnp.exp(local_peak - peak), 'code')]
    dot_general x26 -> x0, matrix products: 135 us -> none  [the longest x8 52.8 us: accumulate(): lax.dot_general(resp, token_block, (((0,), (0,)), ((), ())), preferred_el...]
    pallas_call x0 -> x2, Pallas kernels: none -> 98.3 us  [the longest x1 87.1 us: refit(): pl.pallas_call(refit_kernel, in_specs=[vmem] * 4, out_specs=[vmem] * 2, o...]
    all_gather x1 -> x0, waiting for transfers between devices: 69.9 us -> none  [local(): piece = lax.all_gather(unit_tokens, 'code', axis=0, tiled=True)]
    reduce_scatter x1 -> x0, waiting for transfers between devices: 22 us -> none  [local(): lax.psum_scatter(sums, 'dp', scatter_dimension=0, tiled=True)]
    another operation x12 -> x0, local copies, waits for them, and re-layouts: 18.6 us -> none  [the longest x11 17.1 us: encode(): jax.nn.gelu(jnp.dot(normed, w_in, preferred_element_type=jnp.float32), ap...]
    reduce_sum x11 -> x0, other arithmetic: 17.2 us -> none  [the longest x8 14.3 us: block_stats(): return (peak, jnp.sum(jnp.exp(logits - peak[:, None]), axis=1))]
  transfers between devices with their start and end apart: 2 -> 0, of which waited for: 2 -> 0; matrix products, arithmetic and copies ran while one was open for 1% -> 0% of each run, Pallas kernels for 0% -> 0%
where the time goes in v1:
time: 103 us; the launch traced here: 102 us
  Pallas kernels  98.3 us (95%)
  local copies, waits for them, and re-layouts  3.53 us (3%)
    pallas_call x1, Pallas kernels, refit(): pl.pallas_call(refit_kernel, in_specs=[vmem] * 4, out_specs=[vmem] * 2, o...  87.1 us
    pallas_call x1, Pallas kernels, encode(): pl.pallas_call(encode_kernel, grid=(ff // FT,), in_specs=[pl.BlockSpec((r...  11.1 us
    unnamed x2, local copies, waits for them, and re-layouts  3.53 us

profile of v1, /device:TPU:0, one launch (start us, length us, event | category | flops | bytes accessed | tf_op | source)
XLA Modules:
  0.0 102.4 jit_solution(15748680937763499272)
XLA Ops:
  0.6 11.1 %encode.1.ut_ref = bf16[128,256]{1,0:T(8,128)(2,1)} custom-call(bf16[128,1024]{1,0:T(8,128)(2,1)} %x_ref.1, bf16[1024,4096]{1,0:T(8,128)(2,1)} %win_ref.1, bf16[4096,1024]{1,0:T(8,128)(2,1)} %wout_ref.1, bf16[1024,256]{1,0:T(8,128)(2,1)} %wproj_ref.1), custom_call_target="tpu_custom_call" | custom-call | tf_op jit(solution)/shard_map/encode/pallas_call | solution.py:47
  11.7 87.1 %refit.1 = (f32[1024,256]{1,0:T(8,128)}, f32[8,128]{1,0:T(8,128)}) custom-call(bf16[128,256]{1,0:T(8,128)(2,1)} %encode.1.ut_ref, bf16[4096,256]{1,0:T(8,128)(2,1)} %book_ref.1, f32[128,128]{1,0:T(8,128)} %bitcast.3, f32[32,128]{1,0:T(8,128)} %bitcast.4), custom_call_target="tpu_custom_call" | custom-call | tf_op jit(solution)/shard_map/refit/pallas_call | solution.py:437
  98.9 2.3 %copy.11 = f32[1024,256]{1,0:T(8,128)} copy(f32[1024,256]{1,0:T(8,128)} %get-tuple-element.8) | data formatting | bytes 2097152
  101.2 1.3 %copy.12 = f32[1024]{0:T(1024)} copy(f32[1024]{0:T(1024)} %bitcast.5) | data formatting | bytes 8192

commit v2 on v1

--- a/solution.py
+++ b/solution.py
@@ -11,8 +11,9 @@
 F32 = jnp.float32
 BF16 = jnp.bfloat16
 FT = 512
-CH = 512
+CH = 1024
 CB = 512
+MS = 64
 VMEM_LIMIT = 67043328
 
 
@@ -75,7 +76,7 @@
     ut_ref, book_ref, inv_ref, prior_ref,
     out_ref, mass_ref,
     u_all, codes, p, ls0, ls1, lse, mloc, lx, ly, lz, u2,
-    rc, rcm, rx, rxm, sx, sm, totals,
+    rc, rcm, rx, rxm, sx, sm, totals, wide, macc, mrow, sacc, stage,
     ag_send, ag_recv, st_send, st_recv, rs_send, rs_recv,
 ):
     n_codes, width = book_ref.shape
@@ -330,76 +331,95 @@
         rows = pl.ds(pl.multiple_of(tb * tb_size, tb_size), tb_size)
         tokens = u_all[pl.ds(2 * tb, 2)].reshape(tb_size, width)
         u2[rows, :] = (tokens.astype(F32) * w).astype(BF16)
+        for k in range(2):
+            wide[2 * tb + k] = jnp.broadcast_to(mloc[tb][:, k * 128:(k + 1) * 128], (16, 128)).astype(BF16)
         return 0
 
     lax.fori_loop(0, n_blocks, scale_body, 0)
 
-    ones = jnp.ones((8, 128), F32)
     per = n_codes // 4
     subs = per // CB
 
     def sums_of(first_row):
         r = pl.ds(pl.multiple_of(first_row, CB), CB)
         s = jnp.dot(p[r, :], u2[...], preferred_element_type=F32)
-        acc = jnp.zeros((CB, 128), F32)
-        for j in range(n_blocks * 2):
-            acc = acc + p[r, j * 128:(j + 1) * 128].astype(F32) * mloc[j // 2][:, (j % 2) * 128:(j % 2) * 128 + 128]
-        m = lax.dot_general(
-            ones, acc, (((1,), (1,)), ((), ())), preferred_element_type=F32, precision=lax.Precision.HIGHEST
-        )
-        return s, m
-
-    def reduce_send(src, dst, slot, to):
-        c = pltpu.make_async_remote_copy(
+        for q in range(CB // MS):
+            rq = pl.ds(pl.multiple_of(first_row + q * MS, MS), MS)
+            acc = None
+            for j in range(0, n_blocks * 2, 2):
+                pair = [
+                    p[rq, k * 128:(k + 1) * 128].reshape(MS // 16, 16, 128) * wide[k][None] for k in (j, j + 1)
+                ]
+                v = (pair[0] + pair[1]).astype(F32)
+                acc = v if acc is None else acc + v
+            macc[q * MS:(q + 1) * MS, :] = acc.reshape(MS, 128)
+        col = jnp.broadcast_to(jnp.sum(macc[...], axis=1, keepdims=True), (CB, 128))
+        for k in range(CB // 128):
+            mrow[:, k * 128:(k + 1) * 128] = col[k * 128:(k + 1) * 128, :].T[0:8, :]
+        sacc[...] = s
+
+    def reduce_copy(src, dst, slot, to):
+        return pltpu.make_async_remote_copy(
             src_ref=src, dst_ref=dst, send_sem=rs_send.at[slot], recv_sem=rs_recv.at[slot],
             device_id=to, device_id_type=pl.DeviceIdType.MESH,
         )
-        c.start()
-        return c
-
-    stage = ls0
-
-    for side in range(2):
-        chip = (1 - xlo) if side == 0 else xlo
-        theirs = (chip * 2 + (1 - core)) * per
-        ours = (chip * 2 + core) * per
-
-        def side_body(b, _, side=side, theirs=theirs, ours=ours):
-            slot = side * subs + b
-            rows = pl.ds(pl.multiple_of(slot * CB, CB), CB)
-            s, m = sums_of(theirs + b * CB)
-            stage[rows, :] = s
-            sm[slot] = m
-            c1 = reduce_send(stage.at[rows], rc.at[slot], slot, partner)
-            c2 = reduce_send(sm.at[slot], rcm.at[slot], 4 + slot, partner)
-            s, m = sums_of(ours + b * CB)
-            c1.wait_recv()
-            c2.wait_recv()
-            s = s + rc[slot]
-            m = m + rcm[slot]
-            if side == 0:
-                sx[b] = s.astype(BF16)
-                sm[4 + b] = m
-                reduce_send(sx.at[b], rx.at[b], 8 + b, across)
-                reduce_send(sm.at[4 + b], rxm.at[b], 10 + b, across)
-            else:
-                totals[b] = s
-                sm[4 + subs + b] = m
-            return 0
-
-        lax.fori_loop(0, subs, side_body, 0)
+
+    def to_partner(slot):
+        return [
+            reduce_copy(stage.at[slot], rc.at[slot], slot, partner),
+            reduce_copy(sm.at[slot], rcm.at[slot], 4 + slot, partner),
+        ]
+
+    def to_across(b):
+        return [
+            reduce_copy(sx.at[b], rx.at[b], 8 + b, across),
+            reduce_copy(sm.at[4 + b], rxm.at[b], 10 + b, across),
+        ]
+
+    def chunk(c, _):
+        side = c // (2 * subs)
+        ours = lax.rem(c // subs, 2)
+        b = lax.rem(c, subs)
+        slot = side * subs + b
+        chip = xlo + (1 - side) * (1 - 2 * xlo)
+        owner = chip * 2 + core + (1 - ours) * (1 - 2 * core)
+        sums_of(owner * per + b * CB)
+
+        @pl.when(ours == 0)
+        def _():
+            stage[slot] = sacc[...].astype(BF16)
+            sm[slot] = mrow[...]
+            for cp in to_partner(slot):
+                cp.start()
+
+        @pl.when(ours == 1)
+        def _():
+            for cp in to_partner(slot):
+                cp.wait_recv()
+
+        @pl.when((ours == 1) & (side == 0))
+        def _():
+            sx[b] = (sacc[...] + rc[slot].astype(F32)).astype(BF16)
+            sm[4 + b] = mrow[...] + rcm[slot]
+            for cp in to_across(b):
+                cp.start()
+
+        @pl.when((ours == 1) & (side == 1))
+        def _():
+            totals[b] = sacc[...] + rc[slot].astype(F32)
+            sm[4 + subs + b] = mrow[...] + rcm[slot]
+
+        return 0
+
+    lax.fori_loop(0, 4 * subs, chunk, 0)
 
     def column(row):
         c = jnp.broadcast_to(row, (128, 128)).T
         return jnp.concatenate([c, c], axis=1)
 
     for b in range(subs):
-        pltpu.make_async_remote_copy(
-            src_ref=sx.at[b], dst_ref=rx.at[b], send_sem=rs_send.at[8 + b], recv_sem=rs_recv.at[8 + b],
-            device_id=across, device_id_type=pl.DeviceIdType.MESH).wait_recv()
-        pltpu.make_async_remote_copy(
-            src_ref=sm.at[4 + b], dst_ref=rxm.at[b], send_sem=rs_send.at[10 + b], recv_sem=rs_recv.at[10 + b],
-            device_id=across, device_id_type=pl.DeviceIdType.MESH).wait_recv()
+        for cp in to_across(b):
+            cp.wait_recv()
         m = sm[4 + subs + b] + rxm[b]
         for k in range(CB // 128):
             local = b * CB + k * 128
@@ -413,19 +433,29 @@
             out_ref[local:local + 128, :] = (prior * book + s) / (prior + column(m_row))
 
     for slot in range(2 * subs):
-        pltpu.make_async_remote_copy(
-            src_ref=stage.at[pl.ds(slot * CB, CB)], dst_ref=rc.at[slot], send_sem=rs_send.at[slot],
-            recv_sem=rs_recv.at[slot], device_id=partner, device_id_type=pl.DeviceIdType.MESH).wait_send()
-        pltpu.make_async_remote_copy(
-            src_ref=sm.at[slot], dst_ref=rcm.at[slot], send_sem=rs_send.at[4 + slot],
-            recv_sem=rs_recv.at[4 + slot], device_id=partner, device_id_type=pl.DeviceIdType.MESH).wait_send()
+        for cp in to_partner(slot):
+            cp.wait_send()
     for b in range(subs):
-        pltpu.make_async_remote_copy(
-            src_ref=sx.at[b], dst_ref=rx.at[b], send_sem=rs_send.at[8 + b], recv_sem=rs_recv.at[8 + b],
-            device_id=across, device_id_type=pl.DeviceIdType.MESH).wait_send()
-        pltpu.make_async_remote_copy(
-            src_ref=sm.at[4 + b], dst_ref=rxm.at[b], send_sem=rs_send.at[10 + b], recv_sem=rs_recv.at[10 + b],
-            device_id=across, device_id_type=pl.DeviceIdType.MESH).wait_send()
+        for cp in to_across(b):
+            cp.wait_send()
+
+
+def hand_on_kernel(a_ref, b_ref, a_out, b_out):
+    a_out[...] = a_ref[...]
+    b_out[...] = b_ref[...]
+
+
+def hand_on(a, b):
+    steps = 4
+    rows = a.shape[0] // steps
+    specs = [
+        pl.BlockSpec((rows, a.shape[1]), lambda i: (i, 0)),
+        pl.BlockSpec(b.shape, lambda i: (0, 0)),
+    ]
+    return pl.pallas_call(
+        hand_on_kernel, grid=(steps,), in_specs=specs, out_specs=specs,
+        out_shape=[jax.ShapeDtypeStruct(v.shape, v.dtype) for v in (a, b)], name="hand_on",
+    )(a, b)
 
 
 def refit(unit_tokens, codebook, inv_temp, prior_mass):
@@ -454,13 +484,18 @@
             pltpu.VMEM((4, 16, 1, 256), F32),
             pltpu.VMEM((4, 16, 1, 256), F32),
             pltpu.VMEM((tokens, width), BF16),
-            pltpu.VMEM((2 * subs, CB, width), F32),
+            pltpu.VMEM((2 * subs, CB, width), BF16),
             pltpu.VMEM((2 * subs, 8, CB), F32),
             pltpu.VMEM((subs, CB, width), BF16),
             pltpu.VMEM((subs, 8, CB), F32),
             pltpu.VMEM((subs, CB, width), BF16),
             pltpu.VMEM((4 + 2 * subs, 8, CB), F32),
             pltpu.VMEM((subs, CB, width), F32),
+            pltpu.VMEM((32, 16, 128), BF16),
+            pltpu.VMEM((CB, 128), F32),
+            pltpu.VMEM((8, CB), F32),
+            pltpu.VMEM((CB, width), F32),
+            pltpu.VMEM((2 * subs, CB, width), BF16),
             pltpu.SemaphoreType.DMA((48,)),
             pltpu.SemaphoreType.DMA((64,)),
             pltpu.SemaphoreType.DMA((8,)),
@@ -473,6 +508,7 @@
         ),
         name="refit",
     )(unit_tokens, codebook, inv_temp.reshape(-1, 128), prior_mass.reshape(-1, 128))
+    out, mass = hand_on(out, mass)
     return out, mass.reshape(-1)
 
 

time: 103 us -> 90.7 us (0.88)
  Pallas kernels: 98.3 us -> 89.7 us
  local copies, waits for them, and re-layouts: 3.53 us -> 0 us
    pallas_call x1, Pallas kernels: 87.1 us -> 75.3 us  [refit(): pl.pallas_call(refit_kernel, in_specs=[vmem] * 4, out_specs=[vmem] * 2, o...]
    unnamed x2 -> x0, local copies, waits for them, and re-layouts: 3.53 us -> none
    pallas_call x0 -> x1, Pallas kernels: none -> 3.37 us  [hand_on(): pl.pallas_call(hand_on_kernel, grid=(steps,), in_specs=specs, out_specs=s...]
where the time goes in v2:
time: 90.7 us; the launch traced here: 90.4 us
  Pallas kernels  89.7 us (99%)
    pallas_call x1, Pallas kernels, refit(): pl.pallas_call(refit_kernel, in_specs=[vmem] * 4, out_specs=[vmem] * 2, o...  75.3 us
    pallas_call x1, Pallas kernels, encode(): pl.pallas_call(encode_kernel, grid=(ff // FT,), in_specs=[pl.BlockSpec((r...  11.1 us
    pallas_call x1, Pallas kernels, hand_on(): pl.pallas_call(hand_on_kernel, grid=(steps,), in_specs=specs, out_specs=s...  3.37 us

profile of v2, /device:TPU:0, one launch (start us, length us, event | category | flops | bytes accessed | tf_op | source)
XLA Modules:
  0.0 90.4 jit_solution(6218590549186849621)
XLA Ops:
  0.6 11.1 %encode.1.ut_ref = bf16[128,256]{1,0:T(8,128)(2,1)} custom-call(bf16[128,1024]{1,0:T(8,128)(2,1)} %x_ref.1, bf16[1024,4096]{1,0:T(8,128)(2,1)} %win_ref.1, bf16[4096,1024]{1,0:T(8,128)(2,1)} %wout_ref.1, bf16[1024,256]{1,0:T(8,128)(2,1)} %wproj_ref.1), custom_call_target="tpu_custom_call" | custom-call | tf_op jit(solution)/shard_map/encode/pallas_call | solution.py:48
  11.7 75.3 %refit.1 = (f32[1024,256]{1,0:T(8,128)}, f32[8,128]{1,0:T(8,128)}) custom-call(bf16[128,256]{1,0:T(8,128)(2,1)} %encode.1.ut_ref, bf16[4096,256]{1,0:T(8,128)(2,1)} %book_ref.1, f32[128,128]{1,0:T(8,128)} %bitcast.3, f32[32,128]{1,0:T(8,128)} %bitcast.4), custom_call_target="tpu_custom_call" | custom-call | tf_op jit(solution)/shard_map/refit/pallas_call | solution.py:467
  87.0 3.4 %hand_on.1 = (f32[1024,256]{1,0:T(8,128)}, f32[8,128]{1,0:T(8,128)}) custom-call(f32[1024,256]{1,0:T(8,128)} %get-tuple-element.6.a_ref, f32[8,128]{1,0:T(8,128)} %get-tuple-element.7.b_ref), custom_call_target="tpu_custom_call" | custom-call | tf_op jit(solution)/shard_map/hand_on/pallas_call | solution.py:455
